TPU v7x, 128 devices: a whole 4x4x4 slice. The times are simulated.
128 devices in a mesh: seq: 16 (over z, y_lo, core), section: 8 (over x, y_hi).
Axes of the slice: x: 4, y: 4 (y_hi: 2, y_lo: 2; y = y_hi * 2 + y_lo), z: 4, core: 2. Of those that a mesh axis runs over, the one named last changes fastest.
Arguments:
- query: bfloat16 [8, 6144, 3072], P('section', 'seq'), may hold values from -24 to 24, as said below
- key: bfloat16 [8, 6144, 3072], P('section', 'seq'), may hold values from -24 to 24
- value: bfloat16 [8, 6144, 3072], P('section', 'seq'), may hold values from -6 to 6
- cotangent: bfloat16 [8, 6144, 3072], P('section', 'seq'), may hold values from -96 to 96
- adjacency: int32 [48, 9], P('seq'), may hold values from 0 to 1, as said below
Outputs:
- gradients: bfloat16 [8, 6144, 3, 3072], P('section', 'seq')
Inputs may be any that keep to these rules, and one draw needn't show every extreme that they name: query and key are drawn together. `adjacency`: the tile relation is symmetric: query tile a attends key tile b exactly when query tile b attends key tile a; every tile attends itself.
All inputs are finite; a program needn't handle non-finite values.
Results may differ from a plain program's by a relative error of at most 0.009.
Values may be sent and summed in bfloat16 or wider, within the bound.
A program may use at most 128 MiB of HBM per device.

v0:
```python
import math

import jax
import jax.numpy as jnp
from jax import lax
from jax.sharding import PartitionSpec as P

HD = 128


def from_behind(block, axis, distance):
    devices = range(lax.axis_size(axis))
    route = [((i - distance) % len(devices), i) for i in devices]
    return lax.ppermute(block, axis, route)


def expand_mask(blocks, tile):
    count_rows, count_cols = blocks.shape
    wide = jnp.broadcast_to(blocks[:, None, :, None] > 0, (count_rows, tile, count_cols, tile))
    return wide.reshape(count_rows * tile, count_cols * tile)


def split_heads(matrix, start, group, head_dim):
    piece = lax.dynamic_slice_in_dim(matrix, start, group * head_dim, 1)
    return piece.reshape(matrix.shape[0], group, head_dim)


def masked_scores(queries, keys, mask, scale):
    scores = jnp.einsum("rgc,kgc->grk", queries, keys, preferred_element_type=jnp.float32) * scale
    return jnp.where(mask[None], scores, -jnp.inf)


def value_terms(prob, values, grads_out):
    prob_half = prob.astype(jnp.bfloat16)
    output = jnp.einsum("grk,kgc->rgc", prob_half, values, preferred_element_type=jnp.float32)
    delta = jnp.einsum("rgc,rgc->gr", grads_out.astype(jnp.float32), output)
    return (prob_half, delta)


def score_grads(prob, delta, values, grads_out):
    dprob = jnp.einsum("rgc,kgc->grk", grads_out, values, preferred_element_type=jnp.float32)
    return (prob * (dprob - delta[:, :, None])).astype(jnp.bfloat16)


def put_columns(target, piece, start):
    flat = piece.astype(jnp.bfloat16).reshape(piece.shape[0], piece.shape[1] * piece.shape[2])
    return lax.dynamic_update_slice_in_dim(target, flat, start, 1)


def per_device(query, key, value, cotangent, adjacency):
    queries = query[0]
    keys = key[0]
    values = value[0]
    grads_out = cotangent[0]
    rows, width = queries.shape
    head_dim = HD
    heads = width // head_dim
    group = math.gcd(heads, 4)
    group_width = group * head_dim
    groups = heads // group
    tiles_dev = adjacency.shape[0]
    tile = rows // tiles_dev
    scale = head_dim ** (-0.5)
    own_mask = expand_mask(adjacency, tile)
    blank = jnp.zeros((rows, width), jnp.bfloat16)
    keys_below, values_below = from_behind((keys, values), "seq", 1)
    keys_above, values_above = from_behind((keys, values), "seq", -1)
    window_keys = jnp.concatenate([keys_below, keys, keys_above], 0)
    window_values = jnp.concatenate([values_below, values, values_above], 0)
    blank_window = jnp.zeros((3 * rows, width), jnp.bfloat16)

    def full_step(index, carry):
        grad_query, part_key, part_value = carry
        start = index * group_width
        q_group = split_heads(queries, start, group, head_dim)
        o_group = split_heads(grads_out, start, group, head_dim)
        k_group = split_heads(window_keys, start, group, head_dim)
        v_group = split_heads(window_values, start, group, head_dim)
        scores = masked_scores(q_group, k_group, own_mask, scale)
        top = jnp.max(scores, axis=2)
        weight = jnp.exp(scores - top[:, :, None])
        prob = weight / jnp.sum(weight, axis=2)[:, :, None]
        prob_half, delta = value_terms(prob, v_group, o_group)
        dscore = score_grads(prob, delta, v_group, o_group)
        dquery = (
            jnp.einsum("grk,kgc->rgc", dscore, k_group, preferred_element_type=jnp.float32) * scale
        )
        dkey = (
            jnp.einsum("grk,rgc->kgc", dscore, q_group, preferred_element_type=jnp.float32) * scale
        )
        dvalue = jnp.einsum("grk,rgc->kgc", prob_half, o_group, preferred_element_type=jnp.float32)
        return (
            put_columns(grad_query, dquery, start),
            put_columns(part_key, dkey, start),
            put_columns(part_value, dvalue, start),
        )

    grad_query, part_key, part_value = lax.fori_loop(
        0, groups, full_step, (blank, blank_window, blank_window)
    )
    back_key, back_value = from_behind((part_key[:rows], part_value[:rows]), "seq", -1)
    ahead_key, ahead_value = from_behind((part_key[2 * rows :], part_value[2 * rows :]), "seq", 1)
    grad_key = (
        part_key[rows : 2 * rows].astype(jnp.float32)
        + back_key.astype(jnp.float32)
        + ahead_key.astype(jnp.float32)
    ).astype(jnp.bfloat16)
    grad_value = (
        part_value[rows : 2 * rows].astype(jnp.float32)
        + back_value.astype(jnp.float32)
        + ahead_value.astype(jnp.float32)
    ).astype(jnp.bfloat16)
    packed = jnp.stack([grad_query, grad_key, grad_value], axis=1)[None]
    return from_behind(packed, "section", -1)


def solution(mesh):
    in_specs = (
        P("section", "seq", None),
        P("section", "seq", None),
        P("section", "seq", None),
        P("section", "seq", None),
        P("seq", None),
    )
    out_specs = P("section", "seq", None, None)
    return jax.shard_map(
        per_device, mesh=mesh, in_specs=in_specs, out_specs=out_specs, check_vma=False
    )
```

profile of v0, /device:TPU:1, one launch (start us, length us, event | category | flops | bytes accessed | tf_op | source)
XLA Modules:
  0.0 574.1 jit_solution(13802757288888149777)
XLA Ops:
  0.0 4.3 copy.24
  13.4 4.3 copy.22
  17.7 4.3 copy.23
  22.0 35.6 %collective-permute-done.3 = bf16[384,3072]{0,1:T(8,128)(2,1)} collective-permute-done((bf16[384,3072]{0,1:T(8,128)(2,1)}, bf16[384,3072]{0,1:T(8,128)(2,1)}, u32[]{:S(2)}, u32[]{:S(2)}) %collective-permute-start.3) | collective-permute-done | bytes 2359328 | tf_op jit(solution)/shard_map/ppermute | solution.py:14
  57.6 6.3 %pad_maximum_fusion.1 = bf16[1152,3072]{0,1:T(8,128)(2,1)} fusion(bf16[384,3072]{0,1:T(8,128)(2,1)} %collective-permute-done.3, bf16[384,3072]{0,1:T(8,128)(2,1)} %bitcast.5, bf16[384,3072]{0,1:T(8,128)(2,1)} %collective-permute-done.2), kind=kLoop, calls=%fused_computation.31 | loop fusion | flops 21233664 | bytes 14155776 | tf_op jit(solution)/shard_map/concatenate | solution.py:69
  63.9 44.2 %collective-permute-done.1 = bf16[384,3072]{0,1:T(8,128)(2,1)} collective-permute-done((bf16[384,3072]{0,1:T(8,128)(2,1)S(1)}, bf16[384,3072]{0,1:T(8,128)(2,1)}, u32[]{:S(2)}, u32[]{:S(2)}) %collective-permute-start.1) | collective-permute-done | bytes 2359328 | tf_op jit(solution)/shard_map/ppermute | solution.py:14
  108.1 5.8 %pad_maximum_fusion = bf16[1152,3072]{0,1:T(8,128)(2,1)} fusion(bf16[384,3072]{0,1:T(8,128)(2,1)} %collective-permute-done.1, bf16[384,3072]{0,1:T(8,128)(2,1)S(1)} %bitcast.115, bf16[384,3072]{0,1:T(8,128)(2,1)} %collective-permute-done), kind=kLoop, calls=%fused_computation.30 | loop fusion | flops 21233664 | bytes 14155776 | tf_op jit(solution)/shard_map/concatenate | solution.py:68
  123.1 181.3 %while.18 = (s32[]{:T(128)}, bf16[384,3072]{1,0:T(8,128)(2,1)}, bf16[1152,3072]{1,0:T(8,128)(2,1)}, bf16[1152,3072]{1,0:T(8,128)(2,1)}, bf16[1152,3072]{0,1:T(8,...) while((s32[]{:T(128)}, bf16[384,3072]{1,0:T(8,128)(2,1)}, ...), condition=%wide.region_3.4_spmd.clone, body=%wide.region_0.3_spmd.clone.sunk | while | flops 2738355712 | bytes 100202736 | solution.py:98
  130.1 6.5 %fusion.62 = (f32[4,384]{1,0:T(4,128)S(1)}, f32[4,384,1152]{2,1,0:T(8,128)}) fusion(pred[384,1152]{1,0:T(8,128)(4,1)} %copy.59, bf16[384,4,128]{0,2,1:T(8,128)(2,1)S(1)} %bitcast.108, bf16[1152,4,128]{0,2,1:T(8,128)(2,1)S(1)} %bitcast.104), kind=kOutput, calls=%fused_computation.38.clone.1 | convolution fusion | flops 460063872 | bytes 9099264 | tf_op jit(solution)/shard_map/while/body/eval_jaxpr/sub | solution.py:81
  160.3 6.5 %fusion.62 = (f32[4,384]{1,0:T(4,128)S(1)}, f32[4,384,1152]{2,1,0:T(8,128)}) fusion(pred[384,1152]{1,0:T(8,128)(4,1)} %copy.59, bf16[384,4,128]{0,2,1:T(8,128)(2,1)S(1)} %bitcast.108, bf16[1152,4,128]{0,2,1:T(8,128)(2,1)S(1)} %bitcast.104), kind=kOutput, calls=%fused_computation.38.clone.1 | convolution fusion | flops 460063872 | bytes 9099264 | tf_op jit(solution)/shard_map/while/body/eval_jaxpr/sub | solution.py:81
  166.8 3.9 fusion.63
  190.5 6.5 %fusion.62 = (f32[4,384]{1,0:T(4,128)S(1)}, f32[4,384,1152]{2,1,0:T(8,128)}) fusion(pred[384,1152]{1,0:T(8,128)(4,1)} %copy.59, bf16[384,4,128]{0,2,1:T(8,128)(2,1)S(1)} %bitcast.108, bf16[1152,4,128]{0,2,1:T(8,128)(2,1)S(1)} %bitcast.104), kind=kOutput, calls=%fused_computation.38.clone.1 | convolution fusion | flops 460063872 | bytes 9099264 | tf_op jit(solution)/shard_map/while/body/eval_jaxpr/sub | solution.py:81
  197.0 3.9 fusion.63
  220.7 6.5 %fusion.62 = (f32[4,384]{1,0:T(4,128)S(1)}, f32[4,384,1152]{2,1,0:T(8,128)}) fusion(pred[384,1152]{1,0:T(8,128)(4,1)} %copy.59, bf16[384,4,128]{0,2,1:T(8,128)(2,1)S(1)} %bitcast.108, bf16[1152,4,128]{0,2,1:T(8,128)(2,1)S(1)} %bitcast.104), kind=kOutput, calls=%fused_computation.38.clone.1 | convolution fusion | flops 460063872 | bytes 9099264 | tf_op jit(solution)/shard_map/while/body/eval_jaxpr/sub | solution.py:81
  227.2 3.9 fusion.63
  251.0 6.5 %fusion.62 = (f32[4,384]{1,0:T(4,128)S(1)}, f32[4,384,1152]{2,1,0:T(8,128)}) fusion(pred[384,1152]{1,0:T(8,128)(4,1)} %copy.59, bf16[384,4,128]{0,2,1:T(8,128)(2,1)S(1)} %bitcast.108, bf16[1152,4,128]{0,2,1:T(8,128)(2,1)S(1)} %bitcast.104), kind=kOutput, calls=%fused_computation.38.clone.1 | convolution fusion | flops 460063872 | bytes 9099264 | tf_op jit(solution)/shard_map/while/body/eval_jaxpr/sub | solution.py:81
  281.2 6.5 %fusion.62 = (f32[4,384]{1,0:T(4,128)S(1)}, f32[4,384,1152]{2,1,0:T(8,128)}) fusion(pred[384,1152]{1,0:T(8,128)(4,1)} %copy.59, bf16[384,4,128]{0,2,1:T(8,128)(2,1)S(1)} %bitcast.108, bf16[1152,4,128]{0,2,1:T(8,128)(2,1)S(1)} %bitcast.104), kind=kOutput, calls=%fused_computation.38.clone.1 | convolution fusion | flops 460063872 | bytes 9099264 | tf_op jit(solution)/shard_map/while/body/eval_jaxpr/sub | solution.py:81
  307.2 5.9 %collective-permute-start.6 = (bf16[384,3072]{1,0:T(8,128)(2,1)S(1)}, bf16[384,3072]{1,0:T(8,128)(2,1)S(1)}, u32[]{:S(2)}, u32[]{:S(2)}) collective-permute-start(bf16[384,3072]{1,0:T(8,128)(2,1)S(1)} %get-tuple-element.209), channel_id=1, source_target_pairs={{8,0},{16,8},{24,16},{32,24},{40,32},{48,40},{56,48},{64,56},{72,6... | collective-permute-start | bytes 7077896 | tf_op jit(solution)/shard_map/ppermute | solution.py:14
  315.3 42.3 %collective-permute-done.6 = bf16[384,3072]{1,0:T(8,128)(2,1)S(1)} collective-permute-done((bf16[384,3072]{1,0:T(8,128)(2,1)S(1)}, bf16[384,3072]{1,0:T(8,128)(2,1)S(1)}, u32[]{:S(2)}, u32[]{:S(2)}) %collective-permute-start.6) | collective-permute-done | bytes 2359328 | tf_op jit(solution)/shard_map/ppermute | solution.py:14
  357.6 6.4 %collective-permute-done.7 = bf16[384,3072]{1,0:T(8,128)(2,1)S(1)} collective-permute-done((bf16[384,3072]{1,0:T(8,128)(2,1)S(1)}, bf16[384,3072]{1,0:T(8,128)(2,1)S(1)}, u32[]{:S(2)}, u32[]{:S(2)}) %collective-permute-start.7) | collective-permute-done | bytes 2359328 | tf_op jit(solution)/shard_map/ppermute | solution.py:14
  366.9 41.2 %collective-permute-done.4 = bf16[384,3072]{1,0:T(8,128)(2,1)S(1)} collective-permute-done((bf16[384,3072]{1,0:T(8,128)(2,1)S(1)}, bf16[384,3072]{1,0:T(8,128)(2,1)S(1)}, u32[]{:S(2)}, u32[]{:S(2)}) %collective-permute-start.4) | collective-permute-done | bytes 2359328 | tf_op jit(solution)/shard_map/ppermute | solution.py:14
  408.1 6.4 %collective-permute-done.5 = bf16[384,3072]{1,0:T(8,128)(2,1)S(1)} collective-permute-done((bf16[384,3072]{1,0:T(8,128)(2,1)S(1)}, bf16[384,3072]{1,0:T(8,128)(2,1)S(1)}, u32[]{:S(2)}, u32[]{:S(2)}) %collective-permute-start.5) | collective-permute-done | bytes 2359328 | tf_op jit(solution)/shard_map/ppermute | solution.py:14
  416.7 5.1 collective-permute-start.8
  421.8 149.4 %collective-permute-done.8 = bf16[1,384,3,3072]{3,1,2,0:T(8,128)(2,1)S(1)} collective-permute-done((bf16[1,384,3,3072]{3,1,2,0:T(8,128)(2,1)S(1)}, bf16[1,384,3,3072]{3,1,2,0:T(8,128)(2,1)S(1)}, u32[]{:S(2)}, u32[]{:S(2)}) %collective-permute-start.8) | collective-permute-done | bytes 7077920 | tf_op jit(solution)/shard_map/ppermute | solution.py:14
  (144 shorter events, 161.5 us)
Async XLA Ops:
  4.3 9.1 %copy-start.3 = (s32[3,9]{1,0:T(4,128)S(1)}, s32[3,9]{1,0:T(4,128)}, u32[]{:S(2)}) copy-start(s32[3,9]{1,0:T(4,128)} %param.11) | copy-start | bytes 328
  4.3 53.3 %collective-permute-start.3 = (bf16[384,3072]{0,1:T(8,128)(2,1)}, bf16[384,3072]{0,1:T(8,128)(2,1)}, u32[]{:S(2)}, u32[]{:S(2)}) collective-permute-start(bf16[384,3072]{0,1:T(8,128)(2,1)} %bitcast.5), channel_id=1, source_target_pairs={{8,0},{16,8},{24,16},{32,24},{40,32},{48,40},{56,48},{64,56},{72,6... | collective-permute-start | bytes 7077896 | tf_op jit(solution)/shard_map/ppermute | solution.py:14
  5.7 51.9 %collective-permute-start.2 = (bf16[384,3072]{0,1:T(8,128)(2,1)}, bf16[384,3072]{0,1:T(8,128)(2,1)}, u32[]{:S(2)}, u32[]{:S(2)}) collective-permute-start(bf16[384,3072]{0,1:T(8,128)(2,1)} %bitcast.5), channel_id=1, source_target_pairs={{120,0},{0,8},{8,16},{16,24},{24,32},{32,40},{40,48},{48,56},{56,6... | collective-permute-start | bytes 7077896 | tf_op jit(solution)/shard_map/ppermute | solution.py:14
  10.0 98.2 %collective-permute-start.1 = (bf16[384,3072]{0,1:T(8,128)(2,1)S(1)}, bf16[384,3072]{0,1:T(8,128)(2,1)}, u32[]{:S(2)}, u32[]{:S(2)}) collective-permute-start(bf16[384,3072]{0,1:T(8,128)(2,1)S(1)} %bitcast.113), channel_id=1, source_target_pairs={{8,0},{16,8},{24,16},{32,24},{40,32},{48,40},{56,48},{64,56},{72,6... | collective-permute-start | bytes 7077896 | tf_op jit(solution)/shard_map/ppermute | solution.py:14
  13.3 94.8 %collective-permute-start = (bf16[384,3072]{0,1:T(8,128)(2,1)S(1)}, bf16[384,3072]{0,1:T(8,128)(2,1)}, u32[]{:S(2)}, u32[]{:S(2)}) collective-permute-start(bf16[384,3072]{0,1:T(8,128)(2,1)S(1)} %bitcast.114), channel_id=1, source_target_pairs={{120,0},{0,8},{8,16},{16,24},{24,32},{32,40},{40,48},{48,56},{56,6... | collective-permute-start | bytes 7077896 | tf_op jit(solution)/shard_map/ppermute | solution.py:14
  136.6 5.0 copy-start
  166.8 5.0 copy-start
  197.0 5.0 copy-start
  227.2 5.0 copy-start
  257.5 5.0 copy-start
  287.7 5.0 copy-start
  304.4 8.8 %copy-start.1 = (bf16[1152,3072]{1,0:T(8,128)(2,1)S(1)}, bf16[1152,3072]{1,0:T(8,128)(2,1)}, u32[]{:S(2)}) copy-start(bf16[1152,3072]{1,0:T(8,128)(2,1)} %get-tuple-element.162) | copy-start | bytes 21233668
  307.2 50.4 %collective-permute-start.6 = (bf16[384,3072]{1,0:T(8,128)(2,1)S(1)}, bf16[384,3072]{1,0:T(8,128)(2,1)S(1)}, u32[]{:S(2)}, u32[]{:S(2)}) collective-permute-start(bf16[384,3072]{1,0:T(8,128)(2,1)S(1)} %get-tuple-element.209), channel_id=1, source_target_pairs={{8,0},{16,8},{24,16},{32,24},{40,32},{48,40},{56,48},{64,56},{72,6... | collective-permute-start | bytes 7077896 | tf_op jit(solution)/shard_map/ppermute | solution.py:14
  313.1 50.9 %collective-permute-start.7 = (bf16[384,3072]{1,0:T(8,128)(2,1)S(1)}, bf16[384,3072]{1,0:T(8,128)(2,1)S(1)}, u32[]{:S(2)}, u32[]{:S(2)}) collective-permute-start(bf16[384,3072]{1,0:T(8,128)(2,1)S(1)} %get-tuple-element.210), channel_id=1, source_target_pairs={{120,0},{0,8},{8,16},{16,24},{24,32},{32,40},{40,48},{48,56},{56,6... | collective-permute-start | bytes 7077896 | tf_op jit(solution)/shard_map/ppermute | solution.py:14
  313.5 94.7 %collective-permute-start.4 = (bf16[384,3072]{1,0:T(8,128)(2,1)S(1)}, bf16[384,3072]{1,0:T(8,128)(2,1)S(1)}, u32[]{:S(2)}, u32[]{:S(2)}) collective-permute-start(bf16[384,3072]{1,0:T(8,128)(2,1)S(1)} %get-tuple-element.207), channel_id=1, source_target_pairs={{8,0},{16,8},{24,16},{32,24},{40,32},{48,40},{56,48},{64,56},{72,6... | collective-permute-start | bytes 7077896 | tf_op jit(solution)/shard_map/ppermute | solution.py:14
  314.8 99.7 %collective-permute-start.5 = (bf16[384,3072]{1,0:T(8,128)(2,1)S(1)}, bf16[384,3072]{1,0:T(8,128)(2,1)S(1)}, u32[]{:S(2)}, u32[]{:S(2)}) collective-permute-start(bf16[384,3072]{1,0:T(8,128)(2,1)S(1)} %get-tuple-element.208), channel_id=1, source_target_pairs={{120,0},{0,8},{8,16},{16,24},{24,32},{32,40},{40,48},{48,56},{56,6... | collective-permute-start | bytes 7077896 | tf_op jit(solution)/shard_map/ppermute | solution.py:14
  366.9 48.9 %copy-start.2 = (bf16[384,3072]{1,0:T(8,128)(2,1)S(1)}, bf16[384,3072]{1,0:T(8,128)(2,1)}, u32[]{:S(2)}) copy-start(bf16[384,3072]{1,0:T(8,128)(2,1)} %get-tuple-element.161) | copy-start | bytes 7077892
  416.7 154.4 %collective-permute-start.8 = (bf16[1,384,3,3072]{3,1,2,0:T(8,128)(2,1)S(1)}, bf16[1,384,3,3072]{3,1,2,0:T(8,128)(2,1)S(1)}, u32[]{:S(2)}, u32[]{:S(2)}) collective-permute-start(bf16[1,384,3,3072]{3,1,2,0:T(8,128)(2,1)S(1)} %maximum_bitcast_fusion), channel_id=1, source_target_pairs={{1,0},{2,1},{3,2},{4,3},{5,4},{6,5},{7,6},{0,7},{9,8},{10,9},{11,1... | collective-permute-start | bytes 21233672 | tf_op jit(solution)/shard_map/ppermute | solution.py:14
where the time goes:
time: 579 us; the launch traced here: 574 us
  waiting for transfers between devices  326 us (56%)
  local copies, waits for them, and re-layouts  112 us (19%)
  matrix products  76.8 us (13%)
  other arithmetic  40.2 us (7%)
  starting transfers between devices  18.8 us (3%)
    ppermute x9, waiting for transfers between devices, from_behind(): return lax.ppermute(block, axis, route)  326 us
    sub x6, matrix products, full_step(): weight = jnp.exp(scores - top[:, :, None])  39 us
    dynamic_update_slice x30, local copies, waits for them, and re-layouts, put_columns(): return lax.dynamic_update_slice_in_dim(target, flat, start, 1)  39 us
    dynamic_slice x24, local copies, waits for them, and re-layouts, split_heads(): piece = lax.dynamic_slice_in_dim(matrix, start, group * head_dim, 1)  28.8 us
    convert_element_type x6, other arithmetic, value_terms(): prob_half = prob.astype(jnp.bfloat16)  23.1 us
    unnamed x12, local copies, waits for them, and re-layouts  18.9 us
    ppermute x9, starting transfers between devices, from_behind(): return lax.ppermute(block, axis, route)  18.8 us
  transfers between devices with their start and end apart: 9, of which 7 were waited for; matrix products, arithmetic and copies ran while one was open for 4% of the time, Pallas kernels for 0%

commit v1 on v0

v1 whole, which is shorter than its diff:
```python
import functools
import math

import jax
import jax.numpy as jnp
from jax import lax
from jax.experimental import pallas as pl
from jax.experimental.pallas import tpu as pltpu
from jax.sharding import PartitionSpec as P

HD = 128
QUAD = 4
NEG = -1e30
BF = jnp.bfloat16
F32 = jnp.float32


def dot(a, b, dims):
    return lax.dot_general(a, b, (dims, ((), ())), preferred_element_type=F32)


def kernel(
    q_ref, k_ref, v_ref, o_ref, bias_ref, out_ref,
    kvb, qob, biasb, ob, hs, hr, rl, acc,
    r_kv, r_qo, r_b, r_halo, r_part, r_rl, r_fin,
    s_in, s_b, s_halo, s_part, s_out, s_rl,
    *, rows, own, tile, sections, shards,
):
    nz = shards // QUAD
    seq = lax.axis_index("seq")
    sec = lax.axis_index("section")
    z, g = seq // QUAD, seq % QUAD
    p, c = g // 2, g % 2
    base = z * QUAD
    target = (sec + sections - 1) % sections
    source = (sec + 1) % sections
    other = base + 2 * (1 - p)
    z_prev = ((z + nz - 1) % nz) * QUAD + g
    z_next = ((z + 1) % nz) * QUAD + g
    scale = HD**-0.5
    window = 3 * rows
    mesh_id = pl.DeviceIdType.MESH

    def device(at_seq, at_sec=None):
        return {"seq": at_seq, "section": sec if at_sec is None else at_sec}

    def cols(head):
        return pl.ds(pl.multiple_of(head * HD, HD), HD)

    def slab(slot):
        return pl.ds(pl.multiple_of(slot * rows, rows), rows)

    def send(src, dst, ssem, rsem, to):
        pltpu.make_async_remote_copy(
            src_ref=src, dst_ref=dst, send_sem=ssem, recv_sem=rsem, device_id=to, device_id_type=mesh_id
        ).start()

    def wait(ref, sem):
        pltpu.make_async_copy(ref, ref, sem).wait()

    barrier = pltpu.get_barrier_semaphore()
    partners = [device(base + (g + d) % QUAD) for d in range(1, QUAD)]
    partners += [device(z_prev), device(z_next)]
    partners += [device(other + e, target) for e in range(2)]
    partners += [device(other + e, source) for e in range(2)]
    for to in partners:
        pl.semaphore_signal(barrier, inc=1, device_id=to, device_id_type=mesh_id)
    pl.semaphore_wait(barrier, len(partners))

    for d in range(1, QUAD):
        to = device(base + (g + d) % QUAD)
        send(bias_ref, biasb.at[g], s_b.at[d - 1], r_b.at[g], to)
    pltpu.make_async_copy(bias_ref, biasb.at[g], r_b.at[g]).start()

    def scatter(h, carry):
        mine = cols(g * own + h)
        pltpu.make_async_copy(k_ref.at[:, mine], kvb.at[h, 0, slab(g + 1)], r_kv.at[h, g]).start()
        pltpu.make_async_copy(v_ref.at[:, mine], kvb.at[h, 1, slab(g + 1)], r_kv.at[h, g]).start()
        pltpu.make_async_copy(q_ref.at[:, mine], qob.at[h, 0, slab(g)], r_qo.at[h, g]).start()
        pltpu.make_async_copy(o_ref.at[:, mine], qob.at[h, 1, slab(g)], r_qo.at[h, g]).start()
        for d in (2, 3, 1):
            peer = (g + d) % QUAD
            to = device(base + peer)
            theirs = cols(peer * own + h)
            send(k_ref.at[:, theirs], kvb.at[h, 0, slab(g + 1)], s_in.at[h], r_kv.at[h, g], to)
            send(v_ref.at[:, theirs], kvb.at[h, 1, slab(g + 1)], s_in.at[h], r_kv.at[h, g], to)
        for d in (2, 3, 1):
            peer = (g + d) % QUAD
            to = device(base + peer)
            theirs = cols(peer * own + h)
            send(q_ref.at[:, theirs], qob.at[h, 0, slab(g)], s_in.at[h], r_qo.at[h, g], to)
            send(o_ref.at[:, theirs], qob.at[h, 1, slab(g)], s_in.at[h], r_qo.at[h, g], to)
        return carry

    lax.fori_loop(0, own, scatter, 0)

    def post(h, i, first, count, kind):
        to = device(other + i % 2, target)
        src = ob.at[h, i, pl.ds(first, count)]

        @pl.when(i // 2 != p)
        def _():
            send(src, out_ref.at[pl.ds(first, count), :, cols(g * own + h)], s_out.at[h], r_fin.at[h], to)

        @pl.when(i // 2 == p)
        def _():
            send(src, rl.at[h, c, pl.ds(first, count)], s_out.at[h], r_rl.at[h, c, kind], to)

    def relay(h):
        to = device(other + c)
        for kind, first, count in ((0, 0, 1), (1, 1, 2)):
            for e in range(2):
                block = rl.at[h, e, pl.ds(first, count)]
                wait(block, r_rl.at[h, e, kind])
                head = (2 * (1 - p) + e) * own + h
                send(block, out_ref.at[pl.ds(first, count), :, cols(head)], s_rl.at[h], r_fin.at[h], to)

    def attend(h, i):
        win = pl.ds(pl.multiple_of(i * rows, rows), window)
        keys, values = kvb[h, 0, win, :], kvb[h, 1, win, :]
        queries, grads = qob[h, 0, slab(i), :], qob[h, 1, slab(i), :]
        scores = dot(keys, queries, ((1,), (1,)))
        bias = biasb[i]
        count = window // tile
        scores = jnp.concatenate(
            [scores[j * tile : (j + 1) * tile] + bias[j : j + 1] for j in range(count)], axis=0
        )
        top = jnp.max(scores, axis=0, keepdims=True)
        weight = jnp.exp2((scores - top) * (scale * math.log2(math.e)))
        total = jnp.sum(weight, axis=0, keepdims=True)
        prob = weight * (1.0 / total)
        half = prob.astype(BF)
        dprob = dot(values, grads, ((1,), (1,)))
        delta = jnp.sum(half.astype(F32) * dprob, axis=0, keepdims=True)
        dscore = (prob * (dprob - delta)).astype(BF)
        ob[h, i, 0] = (dot(dscore, keys, ((0,), (0,))) * scale).astype(BF)
        acc[0, win, :] += dot(dscore, queries, ((1,), (0,)))
        acc[1, win, :] += dot(half, grads, ((1,), (0,)))

    for e in range(QUAD):
        wait(bias_ref, r_b.at[e])

    def step(h, carry):
        kv_slot = lambda slot: kvb.at[h, :, slab(slot)]
        wait(kv_slot(1), r_kv.at[h, 0])
        send(kv_slot(1), kv_slot(QUAD + 1), s_halo.at[h, 0], r_halo.at[h, 1], device(z_prev))
        wait(kv_slot(QUAD), r_kv.at[h, QUAD - 1])
        send(kv_slot(QUAD), kv_slot(0), s_halo.at[h, 1], r_halo.at[h, 0], device(z_next))
        acc[...] = jnp.zeros_like(acc)
        for e in range(1, QUAD - 1):
            wait(kv_slot(e + 1), r_kv.at[h, e])
        for e in range(QUAD):
            wait(qob.at[h, :, slab(e)], r_qo.at[h, e])
        wait(kv_slot(0), r_halo.at[h, 0])
        wait(kv_slot(QUAD + 1), r_halo.at[h, 1])

        def query_slot(index, inner):
            i = (3 * index) % QUAD
            attend(h, i)
            post(h, i, 0, 1, 0)

            @pl.when(index == 0)
            def _():
                hs[h, 0, 0] = (acc[0, 0:rows] * scale).astype(BF)
                hs[h, 0, 1] = acc[1, 0:rows].astype(BF)
                send(hs.at[h, 0], hr.at[h, 1], s_part.at[h, 0], r_part.at[h, 1], device(z_prev))

            @pl.when(index == 1)
            def _():
                hs[h, 1, 0] = (acc[0, 5 * rows :] * scale).astype(BF)
                hs[h, 1, 1] = acc[1, 5 * rows :].astype(BF)
                send(hs.at[h, 1], hr.at[h, 0], s_part.at[h, 1], r_part.at[h, 0], device(z_next))

            return inner

        lax.fori_loop(0, QUAD, query_slot, 0)
        for i in (1, 2):
            ob[h, i, 1] = (acc[0, (i + 1) * rows : (i + 2) * rows] * scale).astype(BF)
            ob[h, i, 2] = acc[1, (i + 1) * rows : (i + 2) * rows].astype(BF)
            post(h, jnp.int32(i), 1, 2, 1)
        for side, i in ((0, 0), (1, QUAD - 1)):
            wait(hr.at[h, side], r_part.at[h, side])
            ob[h, i, 1] = (
                acc[0, (i + 1) * rows : (i + 2) * rows] * scale + hr[h, side, 0].astype(F32)
            ).astype(BF)
            ob[h, i, 2] = (acc[1, (i + 1) * rows : (i + 2) * rows] + hr[h, side, 1].astype(F32)).astype(BF)
            post(h, jnp.int32(i), 1, 2, 1)

        @pl.when(h >= LAG)
        def _():
            relay(h - LAG)

        return carry

    lax.fori_loop(0, own, step, 0)

    def tail(h, carry):
        relay(h)
        return carry

    lax.fori_loop(max(own - LAG, 0), own, tail, 0)

    def drain(h, carry):
        wait(ob.at[h], s_in.at[h])
        wait(ob.at[h], s_out.at[h])
        wait(rl.at[h], s_rl.at[h])
        for e in range(2):
            wait(hs.at[h, e], s_halo.at[h, e])
            wait(hs.at[h, e], s_part.at[h, e])
        wait(ob.at[h], r_fin.at[h])
        return carry

    lax.fori_loop(0, own, drain, 0)
    for d in range(QUAD - 1):
        wait(bias_ref, s_b.at[d])


LAG = 2


def per_device(query, key, value, cotangent, adjacency, *, sections, shards):
    _, rows, width = query.shape
    own = width // HD // QUAD
    tiles, links = adjacency.shape
    tile = rows // tiles
    bias = jnp.where(adjacency > 0, 0.0, NEG).astype(F32).T
    bias = jnp.repeat(bias, tile, axis=1)
    bias = jnp.pad(bias, ((0, 16 - links), (0, 0)))
    dma, vmem = pltpu.SemaphoreType.DMA, pltpu.VMEM
    hbm = pl.BlockSpec(memory_space=pltpu.HBM)
    out = pl.pallas_call(
        functools.partial(kernel, rows=rows, own=own, tile=tile, sections=sections, shards=shards),
        out_shape=jax.ShapeDtypeStruct((3, rows, width), BF),
        in_specs=[hbm] * 5,
        out_specs=pl.BlockSpec(memory_space=pl.ANY),
        scratch_shapes=[
            vmem((own, 2, (QUAD + 2) * rows, HD), BF),
            vmem((own, 2, QUAD * rows, HD), BF),
            vmem((QUAD, 16, rows), F32),
            vmem((own, QUAD, 3, rows, HD), BF),
            vmem((own, 2, 2, rows, HD), BF),
            vmem((own, 2, 2, rows, HD), BF),
            vmem((own, 2, 3, rows, HD), BF),
            vmem((2, (QUAD + 2) * rows, HD), F32),
            dma((own, QUAD)),
            dma((own, QUAD)),
            dma((QUAD,)),
            dma((own, 2)),
            dma((own, 2)),
            dma((own, 2, 2)),
            dma((own,)),
            dma((own,)),
            dma((QUAD - 1,)),
            dma((own, 2)),
            dma((own, 2)),
            dma((own,)),
            dma((own,)),
        ],
        compiler_params=pltpu.CompilerParams(
            collective_id=0, has_side_effects=True, vmem_limit_bytes=52 * 1024 * 1024
        ),
    )(query[0], key[0], value[0], cotangent[0], bias)
    return jnp.transpose(out, (1, 0, 2))[None]


def solution(mesh):
    in_specs = (
        P("section", "seq", None),
        P("section", "seq", None),
        P("section", "seq", None),
        P("section", "seq", None),
        P("seq", None),
    )
    out_specs = P("section", "seq", None, None)
    body = functools.partial(per_device, sections=mesh.shape["section"], shards=mesh.shape["seq"])
    return jax.shard_map(body, mesh=mesh, in_specs=in_specs, out_specs=out_specs, check_vma=False)
```

time: 579 us -> 194 us (0.34)
  waiting for transfers between devices: 326 us -> 0 us
  Pallas kernels: 0 us -> 187 us
  local copies, waits for them, and re-layouts: 112 us -> 6.71 us
  matrix products: 76.8 us -> 0 us
  other arithmetic: 40.2 us -> 0.68 us
  starting transfers between devices: 18.8 us -> 0 us
    ppermute x9 -> x0, waiting for transfers between devices: 326 us -> none  [from_behind(): return lax.ppermute(block, axis, route)]
    pallas_call x0 -> x1, Pallas kernels: none -> 187 us  [per_device(): pl.pallas_call(functools.partial(kernel, rows=rows, own=own, tile=tile, s...]
    sub x6 -> x0, matrix products: 39 us -> none  [full_step(): weight = jnp.exp(scores - top[:, :, None])]
    dynamic_update_slice x30 -> x0, local copies, waits for them, and re-layouts: 39 us -> none  [put_columns(): return lax.dynamic_update_slice_in_dim(target, flat, start, 1)]
    dot_general x30 -> x0, matrix products: 37.7 us -> none  [the longest x6 11.3 us: full_step(): jnp.einsum('grk,kgc->rgc', dscore, k_group, preferred_element_type=jnp.fl...]
    dynamic_slice x24 -> x0, local copies, waits for them, and re-layouts: 28.8 us -> none  [split_heads(): piece = lax.dynamic_slice_in_dim(matrix, start, group * head_dim, 1)]
    convert_element_type x6 -> x0, other arithmetic: 23.1 us -> none  [value_terms(): prob_half = prob.astype(jnp.bfloat16)]
    broadcast_in_dim x15 -> x1, local copies, waits for them, and re-layouts: 20.8 us -> 0.07 us  [per_device(): bias = jnp.repeat(bias, tile, axis=1)]
  transfers between devices with their start and end apart: 9 -> 0, of which waited for: 7 -> 0; matrix products, arithmetic and copies ran while one was open for 4% -> 0% of each run, Pallas kernels for 0% -> 0%
where the time goes in v1:
time: 194 us
  Pallas kernels  187 us (96%)
  local copies, waits for them, and re-layouts  6.71 us (3%)
    pallas_call x1, Pallas kernels, per_device(): pl.pallas_call(functools.partial(kernel, rows=rows, own=own, tile=tile, s...  187 us
    unnamed x3, local copies, waits for them, and re-layouts  6.53 us

profile of v1, /device:TPU:1, one launch (start us, length us, event | category | flops | bytes accessed | tf_op | source)
XLA Modules:
  0.0 194.0 jit_solution(17250258350702070586)
XLA Ops:
  0.0 0.7 select_bitcast_fusion
  0.7 0.1 copy.6
  0.8 0.1 broadcast_in_dim.16
  0.9 186.6 %shard_map.55 = bf16[3,384,3072]{2,1,0:T(8,128)(2,1)} custom-call(bf16[384,3072]{1,0:T(8,128)(2,1)} %bitcast.13, bf16[384,3072]{1,0:T(8,128)(2,1)} %bitcast.14, bf16[384,3072]{1,0:T(8,128)(2,1)} %bitcast.15, bf16[384,3072]{1,0:T(8,128)(2,1)} %bitcast.16, f32[16,384]{1,0:T(8,128)S(1)} %pad.4.bias_ref), custom_call_target="tpu_custom_call" | custom-call | tf_op jit(solution)/shard_map/pallas_call | solution.py:231
  187.5 6.5 %copy.9 = bf16[1,384,3,3072]{3,1,2,0:T(8,128)(2,1)} copy(bf16[1,384,3,3072]{3,1,2,0:T(8,128)(2,1)} %bitcast.12) | data formatting | bytes 14155776
  (3 shorter events, 0.0 us)

commit v2 on v1

--- a/solution.py
+++ b/solution.py
@@ -21,7 +21,7 @@
 
 def kernel(
     q_ref, k_ref, v_ref, o_ref, bias_ref, out_ref,
-    kvb, qob, biasb, ob, hs, hr, rl, acc,
+    kvb, qob, rawb, biasb, ob, hs, hr, rl, acc,
     r_kv, r_qo, r_b, r_halo, r_part, r_rl, r_fin,
     s_in, s_b, s_halo, s_part, s_out, s_rl,
     *, rows, own, tile, sections, shards,
@@ -69,8 +69,8 @@
 
     for d in range(1, QUAD):
         to = device(base + (g + d) % QUAD)
-        send(bias_ref, biasb.at[g], s_b.at[d - 1], r_b.at[g], to)
-    pltpu.make_async_copy(bias_ref, biasb.at[g], r_b.at[g]).start()
+        send(bias_ref, rawb.at[g], s_b.at[d - 1], r_b.at[g], to)
+    pltpu.make_async_copy(bias_ref, rawb.at[g], r_b.at[g]).start()
 
     def scatter(h, carry):
         mine = cols(g * own + h)
@@ -78,16 +78,11 @@
         pltpu.make_async_copy(v_ref.at[:, mine], kvb.at[h, 1, slab(g + 1)], r_kv.at[h, g]).start()
         pltpu.make_async_copy(q_ref.at[:, mine], qob.at[h, 0, slab(g)], r_qo.at[h, g]).start()
         pltpu.make_async_copy(o_ref.at[:, mine], qob.at[h, 1, slab(g)], r_qo.at[h, g]).start()
-        for d in (2, 3, 1):
-            peer = (g + d) % QUAD
+        for peer in (2 * (1 - p), 2 * (1 - p) + 1, 2 * p + 1 - c):
             to = device(base + peer)
             theirs = cols(peer * own + h)
             send(k_ref.at[:, theirs], kvb.at[h, 0, slab(g + 1)], s_in.at[h], r_kv.at[h, g], to)
             send(v_ref.at[:, theirs], kvb.at[h, 1, slab(g + 1)], s_in.at[h], r_kv.at[h, g], to)
-        for d in (2, 3, 1):
-            peer = (g + d) % QUAD
-            to = device(base + peer)
-            theirs = cols(peer * own + h)
             send(q_ref.at[:, theirs], qob.at[h, 0, slab(g)], s_in.at[h], r_qo.at[h, g], to)
             send(o_ref.at[:, theirs], qob.at[h, 1, slab(g)], s_in.at[h], r_qo.at[h, g], to)
         return carry
@@ -139,6 +134,12 @@
 
     for e in range(QUAD):
         wait(bias_ref, r_b.at[e])
+        rule = rawb[e]
+        for j in range(window // tile):
+            for n in range(rows // tile):
+                biasb[e, j : j + 1, n * tile : (n + 1) * tile] = jnp.broadcast_to(
+                    rule[n : n + 1, j : j + 1], (1, tile)
+                )
 
     def step(h, carry):
         kv_slot = lambda slot: kvb.at[h, :, slab(slot)]
@@ -149,23 +150,31 @@
         acc[...] = jnp.zeros_like(acc)
         for e in range(1, QUAD - 1):
             wait(kv_slot(e + 1), r_kv.at[h, e])
-        for e in range(QUAD):
-            wait(qob.at[h, :, slab(e)], r_qo.at[h, e])
-        wait(kv_slot(0), r_halo.at[h, 0])
-        wait(kv_slot(QUAD + 1), r_halo.at[h, 1])
 
         def query_slot(index, inner):
-            i = (3 * index) % QUAD
+            half = index // 2
+            first = (1 - index) * (1 - half) + (5 - index) * half
+            i = first + p * (QUAD - 1 - 2 * first)
+            wait(qob.at[h, :, slab(i)], r_qo.at[h, i])
+
+            @pl.when(i == 0)
+            def _():
+                wait(kv_slot(0), r_halo.at[h, 0])
+
+            @pl.when(i == QUAD - 1)
+            def _():
+                wait(kv_slot(QUAD + 1), r_halo.at[h, 1])
+
             attend(h, i)
             post(h, i, 0, 1, 0)
 
-            @pl.when(index == 0)
+            @pl.when(i == 0)
             def _():
                 hs[h, 0, 0] = (acc[0, 0:rows] * scale).astype(BF)
                 hs[h, 0, 1] = acc[1, 0:rows].astype(BF)
                 send(hs.at[h, 0], hr.at[h, 1], s_part.at[h, 0], r_part.at[h, 1], device(z_prev))
 
-            @pl.when(index == 1)
+            @pl.when(i == QUAD - 1)
             def _():
                 hs[h, 1, 0] = (acc[0, 5 * rows :] * scale).astype(BF)
                 hs[h, 1, 1] = acc[1, 5 * rows :].astype(BF)
@@ -174,17 +183,29 @@
             return inner
 
         lax.fori_loop(0, QUAD, query_slot, 0)
-        for i in (1, 2):
-            ob[h, i, 1] = (acc[0, (i + 1) * rows : (i + 2) * rows] * scale).astype(BF)
-            ob[h, i, 2] = acc[1, (i + 1) * rows : (i + 2) * rows].astype(BF)
-            post(h, jnp.int32(i), 1, 2, 1)
-        for side, i in ((0, 0), (1, QUAD - 1)):
-            wait(hr.at[h, side], r_part.at[h, side])
-            ob[h, i, 1] = (
-                acc[0, (i + 1) * rows : (i + 2) * rows] * scale + hr[h, side, 0].astype(F32)
-            ).astype(BF)
-            ob[h, i, 2] = (acc[1, (i + 1) * rows : (i + 2) * rows] + hr[h, side, 1].astype(F32)).astype(BF)
-            post(h, jnp.int32(i), 1, 2, 1)
+
+        def finish(index, inner):
+            half = index // 2
+            first = (1 - index) * (1 - half) + index * half
+            i = first + p * (QUAD - 1 - 2 * first)
+            edge = (i == 0) | (i == QUAD - 1)
+            side = i // (QUAD - 1)
+
+            @pl.when(edge)
+            def _():
+                wait(hr.at[h, side], r_part.at[h, side])
+                ob[h, i, 1] = (acc[0, slab(i + 1)] * scale + hr[h, side, 0].astype(F32)).astype(BF)
+                ob[h, i, 2] = (acc[1, slab(i + 1)] + hr[h, side, 1].astype(F32)).astype(BF)
+
+            @pl.when(jnp.logical_not(edge))
+            def _():
+                ob[h, i, 1] = (acc[0, slab(i + 1)] * scale).astype(BF)
+                ob[h, i, 2] = acc[1, slab(i + 1)].astype(BF)
+
+            post(h, i, 1, 2, 1)
+            return inner
+
+        lax.fori_loop(0, QUAD, finish, 0)
 
         @pl.when(h >= LAG)
         def _():
@@ -215,7 +236,7 @@
         wait(bias_ref, s_b.at[d])
 
 
-LAG = 2
+LAG = 3
 
 
 def per_device(query, key, value, cotangent, adjacency, *, sections, shards):
@@ -223,19 +244,19 @@
     own = width // HD // QUAD
     tiles, links = adjacency.shape
     tile = rows // tiles
-    bias = jnp.where(adjacency > 0, 0.0, NEG).astype(F32).T
-    bias = jnp.repeat(bias, tile, axis=1)
-    bias = jnp.pad(bias, ((0, 16 - links), (0, 0)))
+    bias = jnp.where(adjacency > 0, 0.0, NEG).astype(F32)
+    bias = jnp.pad(bias, ((0, 8 - tiles), (0, HD - links)))
     dma, vmem = pltpu.SemaphoreType.DMA, pltpu.VMEM
     hbm = pl.BlockSpec(memory_space=pltpu.HBM)
     out = pl.pallas_call(
         functools.partial(kernel, rows=rows, own=own, tile=tile, sections=sections, shards=shards),
-        out_shape=jax.ShapeDtypeStruct((3, rows, width), BF),
+        out_shape=pltpu.VMEM((3, rows, width), BF),
         in_specs=[hbm] * 5,
-        out_specs=pl.BlockSpec(memory_space=pl.ANY),
+        out_specs=pl.BlockSpec(memory_space=pltpu.VMEM),
         scratch_shapes=[
             vmem((own, 2, (QUAD + 2) * rows, HD), BF),
             vmem((own, 2, QUAD * rows, HD), BF),
+            vmem((QUAD, 8, HD), F32),
             vmem((QUAD, 16, rows), F32),
             vmem((own, QUAD, 3, rows, HD), BF),
             vmem((own, 2, 2, rows, HD), BF),
@@ -257,7 +278,7 @@
             dma((own,)),
         ],
         compiler_params=pltpu.CompilerParams(
-            collective_id=0, has_side_effects=True, vmem_limit_bytes=52 * 1024 * 1024
+            collective_id=0, has_side_effects=True, vmem_limit_bytes=54 * 1024 * 1024
         ),
     )(query[0], key[0], value[0], cotangent[0], bias)
     return jnp.transpose(out, (1, 0, 2))[None]

time: 194 us -> 190 us (0.979)
  local copies, waits for them, and re-layouts: 6.71 us -> 3.56 us
  Pallas kernels: 187 us -> 185 us
    unnamed x3 -> x1, local copies, waits for them, and re-layouts: 6.53 us -> 2.96 us
where the time goes in v2:
time: 190 us
  Pallas kernels  185 us (97%)
  local copies, waits for them, and re-layouts  3.56 us (2%)
    pallas_call x1, Pallas kernels, per_device(): pl.pallas_call(functools.partial(kernel, rows=rows, own=own, tile=tile, s...  185 us

profile of v2, /device:TPU:1, one launch (start us, length us, event | category | flops | bytes accessed | tf_op | source)
XLA Modules:
  0.0 189.5 jit_solution(17157202595455298255)
XLA Ops:
  0.0 0.7 compare_select_fusion
  0.7 0.6 pad.4.bias_ref
  1.3 185.3 %shard_map.55 = bf16[3,384,3072]{2,1,0:T(8,128)(2,1)S(1)} custom-call(bf16[384,3072]{1,0:T(8,128)(2,1)} %bitcast.8, bf16[384,3072]{1,0:T(8,128)(2,1)} %bitcast.9, bf16[384,3072]{1,0:T(8,128)(2,1)} %bitcast.10, bf16[384,3072]{1,0:T(8,128)(2,1)} %bitcast.11, f32[8,128]{1,0:T(8,128)} %pad.4.bias_ref), custom_call_target="tpu_custom_call" | custom-call | tf_op jit(solution)/shard_map/pallas_call | solution.py:251
  186.6 3.0 %copy.7 = bf16[1,384,3,3072]{3,1,2,0:T(8,128)(2,1)} copy(bf16[1,384,3,3072]{3,1,2,0:T(8,128)(2,1)S(1)} %bitcast.7) | data formatting | bytes 14155776

commit v3 on v2

--- a/solution.py
+++ b/solution.py
@@ -20,10 +20,10 @@
 
 
 def kernel(
-    q_ref, k_ref, v_ref, o_ref, bias_ref, out_ref,
-    kvb, qob, rawb, biasb, ob, hs, hr, rl, acc,
+    q_ref, k_ref, v_ref, o_ref, adj_ref, out_ref,
+    kvb, qob, adjb, biasb, ob, hs, hr, rl, acc,
     r_kv, r_qo, r_b, r_halo, r_part, r_rl, r_fin,
-    s_in, s_b, s_halo, s_part, s_out, s_rl,
+    s_in, s_b, s_halo, s_part, s_out, s_rl, quad_in, near_in,
     *, rows, own, tile, sections, shards,
 ):
     nz = shards // QUAD
@@ -59,18 +59,27 @@
         pltpu.make_async_copy(ref, ref, sem).wait()
 
     barrier = pltpu.get_barrier_semaphore()
-    partners = [device(base + (g + d) % QUAD) for d in range(1, QUAD)]
-    partners += [device(z_prev), device(z_next)]
-    partners += [device(other + e, target) for e in range(2)]
-    partners += [device(other + e, source) for e in range(2)]
-    for to in partners:
-        pl.semaphore_signal(barrier, inc=1, device_id=to, device_id_type=mesh_id)
-    pl.semaphore_wait(barrier, len(partners))
+    for e in (0, 2):
+
+        @pl.when(g != e)
+        def _():
+            pl.semaphore_signal(barrier, inc=1, device_id=device(base + e), device_id_type=mesh_id)
+
+    @pl.when(c == 0)
+    def _():
+        pl.semaphore_wait(barrier, QUAD - 1)
+        pl.semaphore_signal(quad_in, inc=1, device_id=device(base + g + 1), device_id_type=mesh_id)
+        for to in (device(z_prev + 1), device(z_next + 1), device(seq + 1, target), device(seq + 1, source)):
+            pl.semaphore_signal(barrier, inc=1, device_id=to, device_id_type=mesh_id)
+
+    @pl.when(c == 1)
+    def _():
+        pl.semaphore_wait(quad_in, 1)
 
     for d in range(1, QUAD):
         to = device(base + (g + d) % QUAD)
-        send(bias_ref, rawb.at[g], s_b.at[d - 1], r_b.at[g], to)
-    pltpu.make_async_copy(bias_ref, rawb.at[g], r_b.at[g]).start()
+        send(adj_ref, adjb.at[g], s_b.at[d - 1], r_b.at[g], to)
+    pltpu.make_async_copy(adj_ref, adjb.at[g], r_b.at[g]).start()
 
     def scatter(h, carry):
         mine = cols(g * own + h)
@@ -88,6 +97,16 @@
         return carry
 
     lax.fori_loop(0, own, scatter, 0)
+
+    @pl.when(c == 1)
+    def _():
+        pl.semaphore_wait(barrier, 4)
+        pl.semaphore_signal(near_in, inc=1, device_id=device(base + g - 1), device_id_type=mesh_id)
+
+    @pl.when(c == 0)
+    def _():
+        pl.semaphore_wait(near_in, 1)
+
 
     def post(h, i, first, count, kind):
         to = device(other + i % 2, target)
@@ -133,13 +152,12 @@
         acc[1, win, :] += dot(half, grads, ((1,), (0,)))
 
     for e in range(QUAD):
-        wait(bias_ref, r_b.at[e])
-        rule = rawb[e]
+        wait(adj_ref, r_b.at[e])
+        rule = adjb[e]
         for j in range(window // tile):
             for n in range(rows // tile):
-                biasb[e, j : j + 1, n * tile : (n + 1) * tile] = jnp.broadcast_to(
-                    rule[n : n + 1, j : j + 1], (1, tile)
-                )
+                link = jnp.broadcast_to(rule[n : n + 1, j : j + 1], (1, tile))
+                biasb[e, j : j + 1, n * tile : (n + 1) * tile] = jnp.where(link > 0, 0.0, NEG)
 
     def step(h, carry):
         kv_slot = lambda slot: kvb.at[h, :, slab(slot)]
@@ -233,7 +251,7 @@
 
     lax.fori_loop(0, own, drain, 0)
     for d in range(QUAD - 1):
-        wait(bias_ref, s_b.at[d])
+        wait(adj_ref, s_b.at[d])
 
 
 LAG = 3
@@ -244,8 +262,6 @@
     own = width // HD // QUAD
     tiles, links = adjacency.shape
     tile = rows // tiles
-    bias = jnp.where(adjacency > 0, 0.0, NEG).astype(F32)
-    bias = jnp.pad(bias, ((0, 8 - tiles), (0, HD - links)))
     dma, vmem = pltpu.SemaphoreType.DMA, pltpu.VMEM
     hbm = pl.BlockSpec(memory_space=pltpu.HBM)
     out = pl.pallas_call(
@@ -256,7 +272,7 @@
         scratch_shapes=[
             vmem((own, 2, (QUAD + 2) * rows, HD), BF),
             vmem((own, 2, QUAD * rows, HD), BF),
-            vmem((QUAD, 8, HD), F32),
+            vmem((QUAD, tiles, links), jnp.int32),
             vmem((QUAD, 16, rows), F32),
             vmem((own, QUAD, 3, rows, HD), BF),
             vmem((own, 2, 2, rows, HD), BF),
@@ -276,11 +292,13 @@
             dma((own, 2)),
             dma((own,)),
             dma((own,)),
+            pltpu.SemaphoreType.REGULAR,
+            pltpu.SemaphoreType.REGULAR,
         ],
         compiler_params=pltpu.CompilerParams(
             collective_id=0, has_side_effects=True, vmem_limit_bytes=54 * 1024 * 1024
         ),
-    )(query[0], key[0], value[0], cotangent[0], bias)
+    )(query[0], key[0], value[0], cotangent[0], adjacency)
     return jnp.transpose(out, (1, 0, 2))[None]
 
 

time: 190 us -> 186 us (0.979)
  Pallas kernels: 185 us -> 183 us
    pallas_call x1, Pallas kernels: 185 us -> 183 us  [per_device(): pl.pallas_call(functools.partial(kernel, rows=rows, own=own, tile=tile, s...]
where the time goes in v3:
time: 186 us
  Pallas kernels  183 us (98%)
  local copies, waits for them, and re-layouts  2.96 us (2%)
    pallas_call x1, Pallas kernels, per_device(): pl.pallas_call(functools.partial(kernel, rows=rows, own=own, tile=tile, s...  183 us

profile of v3, /device:TPU:1, one launch (start us, length us, event | category | flops | bytes accessed | tf_op | source)
XLA Modules:
  0.0 185.8 jit_solution(3712248615135410765)
XLA Ops:
  0.0 182.8 %shard_map.55 = bf16[3,384,3072]{2,1,0:T(8,128)(2,1)S(1)} custom-call(bf16[384,3072]{1,0:T(8,128)(2,1)} %bitcast.8, bf16[384,3072]{1,0:T(8,128)(2,1)} %bitcast.9, bf16[384,3072]{1,0:T(8,128)(2,1)} %bitcast.10, bf16[384,3072]{1,0:T(8,128)(2,1)} %bitcast.11, s32[3,9]{1,0:T(4,128)} %adj_ref.1), custom_call_target="tpu_custom_call" | custom-call | tf_op jit(solution)/shard_map/pallas_call | solution.py:267
  182.8 3.0 %copy.7 = bf16[1,384,3,3072]{3,1,2,0:T(8,128)(2,1)} copy(bf16[1,384,3,3072]{3,1,2,0:T(8,128)(2,1)S(1)} %bitcast.7) | data formatting | bytes 14155776

commit v4 on v3

--- a/solution.py
+++ b/solution.py
@@ -59,20 +59,20 @@
         pltpu.make_async_copy(ref, ref, sem).wait()
 
     barrier = pltpu.get_barrier_semaphore()
-    for e in (0, 2):
+    for e in (1, 3):
 
         @pl.when(g != e)
         def _():
             pl.semaphore_signal(barrier, inc=1, device_id=device(base + e), device_id_type=mesh_id)
 
-    @pl.when(c == 0)
+    @pl.when(c == 1)
     def _():
         pl.semaphore_wait(barrier, QUAD - 1)
-        pl.semaphore_signal(quad_in, inc=1, device_id=device(base + g + 1), device_id_type=mesh_id)
-        for to in (device(z_prev + 1), device(z_next + 1), device(seq + 1, target), device(seq + 1, source)):
+        pl.semaphore_signal(quad_in, inc=1, device_id=device(base + g - 1), device_id_type=mesh_id)
+        for to in (device(z_prev - 1), device(z_next - 1), device(seq - 1, target), device(seq - 1, source)):
             pl.semaphore_signal(barrier, inc=1, device_id=to, device_id_type=mesh_id)
 
-    @pl.when(c == 1)
+    @pl.when(c == 0)
     def _():
         pl.semaphore_wait(quad_in, 1)
 
@@ -98,15 +98,14 @@
 
     lax.fori_loop(0, own, scatter, 0)
 
+    @pl.when(c == 0)
+    def _():
+        pl.semaphore_wait(barrier, 4)
+        pl.semaphore_signal(near_in, inc=1, device_id=device(base + g + 1), device_id_type=mesh_id)
+
     @pl.when(c == 1)
     def _():
-        pl.semaphore_wait(barrier, 4)
-        pl.semaphore_signal(near_in, inc=1, device_id=device(base + g - 1), device_id_type=mesh_id)
-
-    @pl.when(c == 0)
-    def _():
         pl.semaphore_wait(near_in, 1)
-
 
     def post(h, i, first, count, kind):
         to = device(other + i % 2, target)

time: 186 us -> 185 us (level)
  no operation moved by 1% of the time
where the time goes in v4:
time: 185 us
  Pallas kernels  182 us (98%)
  local copies, waits for them, and re-layouts  2.96 us (2%)
    pallas_call x1, Pallas kernels, per_device(): pl.pallas_call(functools.partial(kernel, rows=rows, own=own, tile=tile, s...  182 us

profile of v4, /device:TPU:1, one launch (start us, length us, event | category | flops | bytes accessed | tf_op | source)
XLA Modules:
  0.0 185.0 jit_solution(15948555301068280036)
XLA Ops:
  0.0 182.0 %shard_map.55 = bf16[3,384,3072]{2,1,0:T(8,128)(2,1)S(1)} custom-call(bf16[384,3072]{1,0:T(8,128)(2,1)} %bitcast.8, bf16[384,3072]{1,0:T(8,128)(2,1)} %bitcast.9, bf16[384,3072]{1,0:T(8,128)(2,1)} %bitcast.10, bf16[384,3072]{1,0:T(8,128)(2,1)} %bitcast.11, s32[3,9]{1,0:T(4,128)} %adj_ref.1), custom_call_target="tpu_custom_call" | custom-call | tf_op jit(solution)/shard_map/pallas_call | solution.py:266
  182.0 3.0 %copy.7 = bf16[1,384,3,3072]{3,1,2,0:T(8,128)(2,1)} copy(bf16[1,384,3,3072]{3,1,2,0:T(8,128)(2,1)S(1)} %bitcast.7) | data formatting | bytes 14155776

commit v5 on v4

--- a/solution.py
+++ b/solution.py
@@ -69,8 +69,6 @@
     def _():
         pl.semaphore_wait(barrier, QUAD - 1)
         pl.semaphore_signal(quad_in, inc=1, device_id=device(base + g - 1), device_id_type=mesh_id)
-        for to in (device(z_prev - 1), device(z_next - 1), device(seq - 1, target), device(seq - 1, source)):
-            pl.semaphore_signal(barrier, inc=1, device_id=to, device_id_type=mesh_id)
 
     @pl.when(c == 0)
     def _():
@@ -78,25 +76,30 @@
 
     for d in range(1, QUAD):
         to = device(base + (g + d) % QUAD)
-        send(adj_ref, adjb.at[g], s_b.at[d - 1], r_b.at[g], to)
-    pltpu.make_async_copy(adj_ref, adjb.at[g], r_b.at[g]).start()
+        send(adj_ref, adjb.at[g], s_b, r_b, to)
+    pltpu.make_async_copy(adj_ref, adjb.at[g], r_b).start()
 
     def scatter(h, carry):
-        mine = cols(g * own + h)
-        pltpu.make_async_copy(k_ref.at[:, mine], kvb.at[h, 0, slab(g + 1)], r_kv.at[h, g]).start()
-        pltpu.make_async_copy(v_ref.at[:, mine], kvb.at[h, 1, slab(g + 1)], r_kv.at[h, g]).start()
-        pltpu.make_async_copy(q_ref.at[:, mine], qob.at[h, 0, slab(g)], r_qo.at[h, g]).start()
-        pltpu.make_async_copy(o_ref.at[:, mine], qob.at[h, 1, slab(g)], r_qo.at[h, g]).start()
         for peer in (2 * (1 - p), 2 * (1 - p) + 1, 2 * p + 1 - c):
             to = device(base + peer)
             theirs = cols(peer * own + h)
-            send(k_ref.at[:, theirs], kvb.at[h, 0, slab(g + 1)], s_in.at[h], r_kv.at[h, g], to)
-            send(v_ref.at[:, theirs], kvb.at[h, 1, slab(g + 1)], s_in.at[h], r_kv.at[h, g], to)
-            send(q_ref.at[:, theirs], qob.at[h, 0, slab(g)], s_in.at[h], r_qo.at[h, g], to)
-            send(o_ref.at[:, theirs], qob.at[h, 1, slab(g)], s_in.at[h], r_qo.at[h, g], to)
+            send(k_ref.at[:, theirs], kvb.at[h, 0, slab(g + 1)], s_in.at[h // 2], r_kv.at[h, p], to)
+            send(v_ref.at[:, theirs], kvb.at[h, 1, slab(g + 1)], s_in.at[h // 2], r_kv.at[h, p], to)
+            send(q_ref.at[:, theirs], qob.at[h, 0, slab(g)], s_in.at[h // 2], r_qo.at[h, p], to)
+            send(o_ref.at[:, theirs], qob.at[h, 1, slab(g)], s_in.at[h // 2], r_qo.at[h, p], to)
+        mine = cols(g * own + h)
+        pltpu.make_async_copy(k_ref.at[:, mine], kvb.at[h, 0, slab(g + 1)], r_kv.at[h, p]).start()
+        pltpu.make_async_copy(v_ref.at[:, mine], kvb.at[h, 1, slab(g + 1)], r_kv.at[h, p]).start()
+        pltpu.make_async_copy(q_ref.at[:, mine], qob.at[h, 0, slab(g)], r_qo.at[h, p]).start()
+        pltpu.make_async_copy(o_ref.at[:, mine], qob.at[h, 1, slab(g)], r_qo.at[h, p]).start()
         return carry
 
     lax.fori_loop(0, own, scatter, 0)
+
+    @pl.when(c == 1)
+    def _():
+        for to in (device(z_prev - 1), device(z_next - 1), device(seq - 1, target), device(seq - 1, source)):
+            pl.semaphore_signal(barrier, inc=1, device_id=to, device_id_type=mesh_id)
 
     @pl.when(c == 0)
     def _():
@@ -113,20 +116,20 @@
 
         @pl.when(i // 2 != p)
         def _():
-            send(src, out_ref.at[pl.ds(first, count), :, cols(g * own + h)], s_out.at[h], r_fin.at[h], to)
+            send(src, out_ref.at[pl.ds(first, count), :, cols(g * own + h)], s_out.at[h // 2], r_fin.at[h // 2], to)
 
         @pl.when(i // 2 == p)
         def _():
-            send(src, rl.at[h, c, pl.ds(first, count)], s_out.at[h], r_rl.at[h, c, kind], to)
+            send(src, rl.at[h, c, pl.ds(first, count)], s_out.at[h // 2], r_rl.at[h, kind], to)
 
     def relay(h):
         to = device(other + c)
         for kind, first, count in ((0, 0, 1), (1, 1, 2)):
+            wait(rl.at[h, :, pl.ds(first, count)], r_rl.at[h, kind])
             for e in range(2):
                 block = rl.at[h, e, pl.ds(first, count)]
-                wait(block, r_rl.at[h, e, kind])
                 head = (2 * (1 - p) + e) * own + h
-                send(block, out_ref.at[pl.ds(first, count), :, cols(head)], s_rl.at[h], r_fin.at[h], to)
+                send(block, out_ref.at[pl.ds(first, count), :, cols(head)], s_rl.at[h // 2], r_fin.at[h // 2], to)
 
     def attend(h, i):
         win = pl.ds(pl.multiple_of(i * rows, rows), window)
@@ -150,8 +153,8 @@
         acc[0, win, :] += dot(dscore, queries, ((1,), (0,)))
         acc[1, win, :] += dot(half, grads, ((1,), (0,)))
 
+    wait(adjb, r_b)
     for e in range(QUAD):
-        wait(adj_ref, r_b.at[e])
         rule = adjb[e]
         for j in range(window // tile):
             for n in range(rows // tile):
@@ -160,27 +163,25 @@
 
     def step(h, carry):
         kv_slot = lambda slot: kvb.at[h, :, slab(slot)]
-        wait(kv_slot(1), r_kv.at[h, 0])
-        send(kv_slot(1), kv_slot(QUAD + 1), s_halo.at[h, 0], r_halo.at[h, 1], device(z_prev))
-        wait(kv_slot(QUAD), r_kv.at[h, QUAD - 1])
-        send(kv_slot(QUAD), kv_slot(0), s_halo.at[h, 1], r_halo.at[h, 0], device(z_next))
+        wait(kvb.at[h, :, pl.ds(rows, 2 * rows)], r_kv.at[h, 0])
+        send(kv_slot(1), kv_slot(QUAD + 1), s_halo, r_halo.at[h], device(z_prev))
+        wait(kvb.at[h, :, pl.ds(3 * rows, 2 * rows)], r_kv.at[h, 1])
+        send(kv_slot(QUAD), kv_slot(0), s_halo, r_halo.at[h], device(z_next))
         acc[...] = jnp.zeros_like(acc)
-        for e in range(1, QUAD - 1):
-            wait(kv_slot(e + 1), r_kv.at[h, e])
 
         def query_slot(index, inner):
             half = index // 2
             first = (1 - index) * (1 - half) + (5 - index) * half
             i = first + p * (QUAD - 1 - 2 * first)
-            wait(qob.at[h, :, slab(i)], r_qo.at[h, i])
-
-            @pl.when(i == 0)
-            def _():
-                wait(kv_slot(0), r_halo.at[h, 0])
-
-            @pl.when(i == QUAD - 1)
-            def _():
-                wait(kv_slot(QUAD + 1), r_halo.at[h, 1])
+            side = half + p * (1 - 2 * half)
+
+            @pl.when(index % 2 == 0)
+            def _():
+                wait(qob.at[h, :, pl.ds(pl.multiple_of(side * 2 * rows, 2 * rows), 2 * rows)], r_qo.at[h, side])
+
+            @pl.when(index == 1)
+            def _():
+                wait(kvb.at[h, :, pl.ds(0, 2 * rows)], r_halo.at[h])
 
             attend(h, i)
             post(h, i, 0, 1, 0)
@@ -189,17 +190,19 @@
             def _():
                 hs[h, 0, 0] = (acc[0, 0:rows] * scale).astype(BF)
                 hs[h, 0, 1] = acc[1, 0:rows].astype(BF)
-                send(hs.at[h, 0], hr.at[h, 1], s_part.at[h, 0], r_part.at[h, 1], device(z_prev))
+                send(hs.at[h, 0], hr.at[h, 1], s_part, r_part.at[h], device(z_prev))
 
             @pl.when(i == QUAD - 1)
             def _():
                 hs[h, 1, 0] = (acc[0, 5 * rows :] * scale).astype(BF)
                 hs[h, 1, 1] = acc[1, 5 * rows :].astype(BF)
-                send(hs.at[h, 1], hr.at[h, 0], s_part.at[h, 1], r_part.at[h, 0], device(z_next))
+                send(hs.at[h, 1], hr.at[h, 0], s_part, r_part.at[h], device(z_next))
 
             return inner
 
         lax.fori_loop(0, QUAD, query_slot, 0)
+
+        wait(hr.at[h], r_part.at[h])
 
         def finish(index, inner):
             half = index // 2
@@ -210,7 +213,6 @@
 
             @pl.when(edge)
             def _():
-                wait(hr.at[h, side], r_part.at[h, side])
                 ob[h, i, 1] = (acc[0, slab(i + 1)] * scale + hr[h, side, 0].astype(F32)).astype(BF)
                 ob[h, i, 2] = (acc[1, slab(i + 1)] + hr[h, side, 1].astype(F32)).astype(BF)
 
@@ -238,19 +240,19 @@
 
     lax.fori_loop(max(own - LAG, 0), own, tail, 0)
 
-    def drain(h, carry):
-        wait(ob.at[h], s_in.at[h])
-        wait(ob.at[h], s_out.at[h])
-        wait(rl.at[h], s_rl.at[h])
-        for e in range(2):
-            wait(hs.at[h, e], s_halo.at[h, e])
-            wait(hs.at[h, e], s_part.at[h, e])
-        wait(ob.at[h], r_fin.at[h])
+    wait(hs, s_halo)
+    wait(hs, s_part)
+    wait(adjb.at[pl.ds(0, QUAD - 1)], s_b)
+
+    def drain(pair, carry):
+        heads = pl.ds(2 * pair, 2)
+        wait(ob.at[heads], s_in.at[pair])
+        wait(ob.at[heads], s_out.at[pair])
+        wait(rl.at[heads], s_rl.at[pair])
+        wait(ob.at[heads], r_fin.at[pair])
         return carry
 
-    lax.fori_loop(0, own, drain, 0)
-    for d in range(QUAD - 1):
-        wait(adj_ref, s_b.at[d])
+    lax.fori_loop(0, own // 2, drain, 0)
 
 
 LAG = 3
@@ -278,19 +280,19 @@
             vmem((own, 2, 2, rows, HD), BF),
             vmem((own, 2, 3, rows, HD), BF),
             vmem((2, (QUAD + 2) * rows, HD), F32),
-            dma((own, QUAD)),
-            dma((own, QUAD)),
-            dma((QUAD,)),
             dma((own, 2)),
             dma((own, 2)),
-            dma((own, 2, 2)),
+            dma,
             dma((own,)),
             dma((own,)),
-            dma((QUAD - 1,)),
             dma((own, 2)),
-            dma((own, 2)),
-            dma((own,)),
-            dma((own,)),
+            dma((own // 2,)),
+            dma((own // 2,)),
+            dma,
+            dma,
+            dma,
+            dma((own // 2,)),
+            dma((own // 2,)),
             pltpu.SemaphoreType.REGULAR,
             pltpu.SemaphoreType.REGULAR,
         ],

time: 185 us -> 184 us (level)
  no operation moved by 1% of the time
where the time goes in v5:
time: 184 us
  Pallas kernels  181 us (98%)
  local copies, waits for them, and re-layouts  2.96 us (2%)
    pallas_call x1, Pallas kernels, per_device(): pl.pallas_call(functools.partial(kernel, rows=rows, own=own, tile=tile, s...  181 us

profile of v5, /device:TPU:1, one launch (start us, length us, event | category | flops | bytes accessed | tf_op | source)
XLA Modules:
  0.0 183.6 jit_solution(8894710533290287675)
XLA Ops:
  0.0 180.6 %shard_map.55 = bf16[3,384,3072]{2,1,0:T(8,128)(2,1)S(1)} custom-call(bf16[384,3072]{1,0:T(8,128)(2,1)} %bitcast.8, bf16[384,3072]{1,0:T(8,128)(2,1)} %bitcast.9, bf16[384,3072]{1,0:T(8,128)(2,1)} %bitcast.10, bf16[384,3072]{1,0:T(8,128)(2,1)} %bitcast.11, s32[3,9]{1,0:T(4,128)} %adj_ref.1), custom_call_target="tpu_custom_call" | custom-call | tf_op jit(solution)/shard_map/pallas_call | solution.py:268
  180.6 3.0 %copy.7 = bf16[1,384,3,3072]{3,1,2,0:T(8,128)(2,1)} copy(bf16[1,384,3,3072]{3,1,2,0:T(8,128)(2,1)S(1)} %bitcast.7) | data formatting | bytes 14155776
